TPU v7x, 32 devices: a whole 2x2x4 slice. The times are simulated.
32 devices in a mesh: fsdp: 32 (over z, y, x, core).
Axes of the slice: x: 2, y: 2, z: 4, core: 2. Of those that a mesh axis runs over, the one named last changes fastest.
Arguments:
- tokens: bfloat16 [16384, 1024], P('fsdp'), may hold values from -6 to 6
- attention_gain: float32 [1024], P('fsdp'), may hold values from 0.5 to 1.5
- query_weight: float32 [1024, 1024], P('fsdp'), may hold values from -0.09375 to 0.09375
- key_weight: float32 [1024, 1024], P('fsdp'), may hold values from -0.09375 to 0.09375
- value_weight: float32 [1024, 1024], P('fsdp'), may hold values from -0.1875 to 0.1875
- output_weight: float32 [1024, 1024], P('fsdp'), may hold values from -0.5 to 0.5
- feedforward_gain: float32 [1024], P('fsdp'), may hold values from 0.5 to 1.5
- inner_weight: float32 [1024, 4096], P('fsdp'), may hold values from -0.1875 to 0.1875
- outer_weight: float32 [4096, 1024], P('fsdp'), may hold values from -0.125 to 0.125
- bias_table: float32 [32, 16], replicated, may hold values from -4 to 4
- segment_ids: int32 [16384], P('fsdp'), may hold values from 0 to 255, as said below
- positions: int32 [16384], P('fsdp'), may hold values from 0 to 255, as said below
- cotangent: bfloat16 [16384, 1024], P('fsdp'), may hold values from -6 to 6
Outputs:
- layer_output: bfloat16 [16384, 1024], P('fsdp')
- tokens_gradient: bfloat16 [16384, 1024], P('fsdp')
- attention_gain_gradient: float32 [1024], P('fsdp')
- query_gradient: float32 [1024, 1024], P('fsdp')
- key_gradient: float32 [1024, 1024], P('fsdp')
- value_gradient: float32 [1024, 1024], P('fsdp')
- output_gradient: float32 [1024, 1024], P('fsdp')
- feedforward_gain_gradient: float32 [1024], P('fsdp')
- inner_gradient: float32 [1024, 4096], P('fsdp')
- outer_gradient: float32 [4096, 1024], P('fsdp')
- table_gradient: float32 [32, 16], replicated
Inputs may be any that keep to these rules, and one draw needn't show every extreme that they name: `segment_ids`: in each packed sequence of 256 consecutive tokens the number starts at 0 and rises by 0 or 1 from one token to the next. In the last packed sequence every token is a document of its own. `positions`: the number of tokens since the start of the token's document; a document starts at the start of each packed sequence and wherever segment_ids rises. The first packed sequence is one whole document.
All inputs are finite; a program needn't handle non-finite values.
Results may differ from a plain program's by a relative error of at most 0.013.
The roundings to bfloat16 on the way count: a program that leaves them out, or rounds other values in their place, can miss the bound.
Values may be sent and summed in bfloat16 or wider, within the bound.
No kernel may reach another device: no remote copies, remote signals or barrier semaphores. Data moves between devices by JAX's collectives and lax.ppermute only.
A program may use at most 192 MiB of HBM per device.

v0:
```python
import math

import jax
import jax.numpy as jnp
from jax import lax
from jax.sharding import PartitionSpec as P

HEADS = 16
HEAD = 64
NB = 32
SEQ = 256
MICRO = 2


EPSILON = 1e-06
MASKED = -1000000000.0
LIMITS = (12, 16, 23, 32, 46, 64, 91)
HIGHEST = lax.Precision.HIGHEST


def bucket_of(relative):
    distance = jnp.abs(relative)
    counted = jnp.zeros_like(distance)
    for threshold in LIMITS:
        counted = counted + (distance >= threshold).astype(jnp.int32)
    inside = jnp.where(distance < 8, distance, 8 + counted)
    return inside + jnp.where(relative > 0, 16, 0).astype(jnp.int32)


def gelu_slope(values):
    normal_cdf = 0.5 * (1.0 + jax.scipy.special.erf(values * (1.0 / math.sqrt(2.0))))
    return normal_cdf + values * jnp.exp(-0.5 * values * values) * (1.0 / math.sqrt(2.0 * math.pi))


def pair_layout(segments, places, bias_table):
    length = segments.shape[1]
    allowed = segments[:, :, None] == segments[:, None, :]
    relative = places[:, None, :] - places[:, :, None]
    offsets = jnp.arange(2 * length - 1, dtype=jnp.int32) - (length - 1)
    lookup = (bucket_of(offsets)[:, None] == jnp.arange(NB, dtype=jnp.int32)[None, :]).astype(
        jnp.float32
    )
    distance_table = jnp.dot(lookup, bias_table, precision=HIGHEST)
    biases = jnp.take(distance_table, relative + (length - 1), axis=0)
    return (allowed, relative, jnp.moveaxis(biases, 3, 1))


def attention_scores(queries, key_rows, allowed, biases):
    scores = (
        jnp.einsum("sqhe,skhe->shqk", queries, key_rows, preferred_element_type=jnp.float32)
        + biases
    )
    return jnp.where(allowed[:, None], scores, MASKED)


def forward_micro(token_rows, segments, places, attention_set, feedforward_set, bias_table):
    query_full, key_full, value_full, output_full, gain_one = attention_set
    inner_full, outer_full, gain_two = feedforward_set
    row_count, width = token_rows.shape
    seq_count, length = segments.shape
    inputs = token_rows.astype(jnp.float32)
    scale_one = lax.rsqrt(jnp.mean(inputs * inputs, axis=-1, keepdims=True) + EPSILON)
    normed_one = (inputs * scale_one * gain_one.astype(jnp.float32)).astype(jnp.bfloat16)

    def project(weight):
        made = jnp.dot(normed_one, weight, preferred_element_type=jnp.float32)
        return made.astype(jnp.bfloat16).reshape(seq_count, length, HEADS, HEAD)

    queries = project(query_full)
    key_rows = project(key_full)
    value_rows = project(value_full)
    allowed, relative, biases = pair_layout(segments, places, bias_table)
    scores = attention_scores(queries, key_rows, allowed, biases)
    row_top = jnp.max(scores, axis=-1, keepdims=True)
    exponent = jnp.exp(scores - row_top)
    row_totals = jnp.sum(exponent, axis=-1, keepdims=True)
    softmax_rows = exponent / row_totals
    log_totals = row_top + jnp.log(row_totals)
    context = jnp.einsum(
        "shqk,skhe->sqhe",
        softmax_rows.astype(jnp.bfloat16),
        value_rows,
        preferred_element_type=jnp.float32,
    )
    context = context.reshape(row_count, width).astype(jnp.bfloat16)
    middle = inputs + jnp.dot(context, output_full, preferred_element_type=jnp.float32)
    scale_two = lax.rsqrt(jnp.mean(middle * middle, axis=-1, keepdims=True) + EPSILON)
    normed_two = (middle * scale_two * gain_two.astype(jnp.float32)).astype(jnp.bfloat16)
    inner_rows = jnp.dot(normed_two, inner_full, preferred_element_type=jnp.float32)
    hidden = jax.nn.gelu(inner_rows, approximate=False).astype(jnp.bfloat16)
    result = (middle + jnp.dot(hidden, outer_full, preferred_element_type=jnp.float32)).astype(
        jnp.bfloat16
    )
    kept_state = (
        inputs,
        scale_one,
        normed_one,
        queries,
        key_rows,
        value_rows,
        log_totals,
        context,
        middle,
        scale_two,
        normed_two,
        inner_rows,
        hidden,
        allowed,
        relative,
        biases,
    )
    return (result, kept_state)


def backward_micro(kept_state, upstream, attention_set, feedforward_set):
    (
        inputs,
        scale_one,
        normed_one,
        queries,
        key_rows,
        value_rows,
        log_totals,
        context,
        middle,
        scale_two,
        normed_two,
        inner_rows,
        hidden,
        allowed,
        relative,
        biases,
    ) = kept_state
    query_full, key_full, value_full, output_full, gain_one = attention_set
    inner_full, outer_full, gain_two = feedforward_set
    row_count, width = upstream.shape
    upstream_float = upstream.astype(jnp.float32)
    outer_grad = jnp.dot(hidden.T, upstream, preferred_element_type=jnp.float32)
    hidden_grad = jnp.dot(upstream, outer_full.T, preferred_element_type=jnp.float32)
    inner_act_grad = (hidden_grad * gelu_slope(inner_rows)).astype(jnp.bfloat16)
    inner_grad = jnp.dot(normed_two.T, inner_act_grad, preferred_element_type=jnp.float32)
    normed_two_grad = jnp.dot(inner_act_grad, inner_full.T, preferred_element_type=jnp.float32)
    gain_two_float = gain_two.astype(jnp.float32)
    gain_two_grad = jnp.sum(normed_two_grad * (middle * scale_two), axis=0)
    cubed_two = scale_two * scale_two * scale_two
    middle_grad = (
        upstream_float
        + scale_two * gain_two_float * normed_two_grad
        - middle
        * cubed_two
        * jnp.mean(middle * gain_two_float * normed_two_grad, axis=-1, keepdims=True)
    )
    attended_grad = middle_grad.astype(jnp.bfloat16)
    output_grad = jnp.dot(context.T, attended_grad, preferred_element_type=jnp.float32)
    context_grad = jnp.dot(attended_grad, output_full.T, preferred_element_type=jnp.float32).astype(
        jnp.bfloat16
    )
    context_grad = context_grad.reshape(queries.shape)
    scores = attention_scores(queries, key_rows, allowed, biases)
    softmax_rows = jnp.exp(scores - log_totals)
    softmax_low = softmax_rows.astype(jnp.bfloat16)
    value_grad_rows = jnp.einsum(
        "shqk,sqhe->skhe", softmax_low, context_grad, preferred_element_type=jnp.float32
    ).astype(jnp.bfloat16)
    softmax_grad = jnp.einsum(
        "sqhe,skhe->shqk", context_grad, value_rows, preferred_element_type=jnp.float32
    )
    inner_sum = jnp.sum(softmax_rows * softmax_grad, axis=-1, keepdims=True)
    score_grad = (softmax_rows * (softmax_grad - inner_sum)).astype(jnp.bfloat16)
    onehot = (bucket_of(relative)[..., None] == jnp.arange(NB, dtype=jnp.int32)).astype(
        jnp.bfloat16
    )
    table_grad = jnp.einsum("sqkb,shqk->bh", onehot, score_grad, preferred_element_type=jnp.float32)
    query_grad_rows = (
        jnp.einsum("shqk,skhe->sqhe", score_grad, key_rows, preferred_element_type=jnp.float32)
        .astype(jnp.bfloat16)
        .reshape(row_count, width)
    )
    key_grad_rows = (
        jnp.einsum("shqk,sqhe->skhe", score_grad, queries, preferred_element_type=jnp.float32)
        .astype(jnp.bfloat16)
        .reshape(row_count, width)
    )
    value_grad_rows = value_grad_rows.reshape(row_count, width)
    query_grad = jnp.dot(normed_one.T, query_grad_rows, preferred_element_type=jnp.float32)
    key_grad = jnp.dot(normed_one.T, key_grad_rows, preferred_element_type=jnp.float32)
    value_grad = jnp.dot(normed_one.T, value_grad_rows, preferred_element_type=jnp.float32)
    normed_one_grad = jnp.dot(query_grad_rows, query_full.T, preferred_element_type=jnp.float32)
    normed_one_grad = normed_one_grad + jnp.dot(
        key_grad_rows, key_full.T, preferred_element_type=jnp.float32
    )
    normed_one_grad = normed_one_grad + jnp.dot(
        value_grad_rows, value_full.T, preferred_element_type=jnp.float32
    )
    gain_one_float = gain_one.astype(jnp.float32)
    gain_one_grad = jnp.sum(normed_one_grad * (inputs * scale_one), axis=0)
    cubed_one = scale_one * scale_one * scale_one
    input_grad = (
        middle_grad
        + scale_one * gain_one_float * normed_one_grad
        - inputs
        * cubed_one
        * jnp.mean(inputs * gain_one_float * normed_one_grad, axis=-1, keepdims=True)
    )
    weight_grads = (
        query_grad,
        key_grad,
        value_grad,
        output_grad,
        gain_one_grad,
        inner_grad,
        outer_grad,
        gain_two_grad,
    )
    return (input_grad.astype(jnp.bfloat16), weight_grads, table_grad)


def per_device(
    tokens,
    attention_gain,
    query_weight,
    key_weight,
    value_weight,
    output_weight,
    feedforward_gain,
    inner_weight,
    outer_weight,
    bias_table,
    segment_ids,
    positions,
    cotangent,
):
    rows_total = tokens.shape[0]
    block_rows = rows_total // MICRO
    block_seqs = block_rows // SEQ
    attention_shards = (
        query_weight.astype(jnp.bfloat16),
        key_weight.astype(jnp.bfloat16),
        value_weight.astype(jnp.bfloat16),
        output_weight.astype(jnp.bfloat16),
        attention_gain.astype(jnp.bfloat16),
    )
    feedforward_shards = (
        inner_weight.astype(jnp.bfloat16),
        outer_weight.astype(jnp.bfloat16),
        feedforward_gain.astype(jnp.bfloat16),
    )

    def weight_sets():
        return (
            (
                lax.all_gather(attention_shards[0], "fsdp", axis=0, tiled=True),
                lax.all_gather(attention_shards[1], "fsdp", axis=0, tiled=True),
                lax.all_gather(attention_shards[2], "fsdp", axis=0, tiled=True),
                lax.all_gather(attention_shards[3], "fsdp", axis=0, tiled=True),
                lax.all_gather(attention_shards[4], "fsdp", axis=0, tiled=True),
            ),
            (
                lax.all_gather(feedforward_shards[0], "fsdp", axis=0, tiled=True),
                lax.all_gather(feedforward_shards[1], "fsdp", axis=0, tiled=True),
                lax.all_gather(feedforward_shards[2], "fsdp", axis=0, tiled=True),
            ),
        )

    def block_slice(array, micro_index):
        return lax.slice_in_dim(
            array, micro_index * block_rows, (micro_index + 1) * block_rows, axis=0
        )

    output_blocks = []
    saved_states = []
    for micro_index in range(MICRO):
        token_rows = block_slice(tokens, micro_index)
        segments = block_slice(segment_ids, micro_index).reshape(block_seqs, SEQ)
        places = block_slice(positions, micro_index).reshape(block_seqs, SEQ)
        attention_set, feedforward_set = weight_sets()
        result, kept_state = forward_micro(
            token_rows, segments, places, attention_set, feedforward_set, bias_table
        )
        output_blocks.append(result)
        saved_states.append(kept_state)
    gradient_blocks = [None] * MICRO
    table_total = jnp.zeros((NB, HEADS), jnp.float32)
    totals = None
    owned_sums = None
    for micro_index in reversed(range(MICRO)):
        attention_set, feedforward_set = weight_sets()
        input_rows, weight_grads, table_grad = backward_micro(
            saved_states[micro_index],
            block_slice(cotangent, micro_index),
            attention_set,
            feedforward_set,
        )
        gradient_blocks[micro_index] = input_rows
        table_total = table_total + table_grad
        totals = weight_grads if totals is None else jax.tree.map(jnp.add, totals, weight_grads)
    owned_sums = lax.psum_scatter(totals, "fsdp", scatter_dimension=0, tiled=True)
    table_sum = lax.psum(table_total, "fsdp")
    layer_output = jnp.concatenate(output_blocks, axis=0)
    tokens_gradient = jnp.concatenate(gradient_blocks, axis=0)
    return (
        layer_output,
        tokens_gradient,
        owned_sums[4],
        owned_sums[0],
        owned_sums[1],
        owned_sums[2],
        owned_sums[3],
        owned_sums[7],
        owned_sums[5],
        owned_sums[6],
        table_sum,
    )


def solution(mesh):
    placed = (
        P("fsdp", None),
        P("fsdp"),
        P("fsdp", None),
        P("fsdp", None),
        P("fsdp", None),
        P("fsdp", None),
        P("fsdp"),
        P("fsdp", None),
        P("fsdp", None),
        P(),
        P("fsdp"),
        P("fsdp"),
        P("fsdp", None),
    )
    return jax.shard_map(
        per_device,
        mesh=mesh,
        in_specs=placed,
        out_specs=(
            P("fsdp", None),
            P("fsdp", None),
            P("fsdp"),
            P("fsdp", None),
            P("fsdp", None),
            P("fsdp", None),
            P("fsdp", None),
            P("fsdp"),
            P("fsdp", None),
            P("fsdp", None),
            P(),
        ),
        check_vma=False,
    )
```

profile of v0, /device:TPU:0, one launch (start us, length us, event | category | flops | bytes accessed | tf_op | source)
XLA Modules:
  0.0 1585.9 jit_solution(4731638638244409950)
XLA Ops:
  19.1 42.0 %all-reduce.5 = (bf16[1024]{0:T(1024)(128)(2,1)S(1)}, bf16[1024]{0:T(1024)(128)(2,1)S(1)}) all-reduce(bf16[1024]{0:T(1024)(128)(2,1)S(1)} %dynamic-update-slice, bf16[1024]{0:T(1024)(128)(2,1)S(1)} %dynamic-update-slice.1), channel_id=1, replica_groups=mesh['fsdp'=32] {'fsdp'}, use_global_device_ids=true, to_apply=%add | all-reduce | flops 2048 | bytes 8192
  63.2 215.9 %gather_fusion.1 = f32[65536,16]{1,0:T(8,128)} fusion(f32[511,16]{1,0:T(8,128)S(1)} %fusion.139, s32[65536]{0:T(1024)S(1)} %broadcast_clamp_fusion), kind=kCustom, calls=%fused_computation.1.clone | custom fusion | bytes 8650752 | tf_op jit(solution)/shard_map/jit(_take)/gather | solution.py:44
  279.2 20.3 %copy.92 = f32[1,256,256,16]{1,2,3,0:T(8,128)} copy(f32[1,256,256,16]{3,2,1,0:T(8,128)} %bitcast.192) | data formatting | bytes 8388608 | tf_op jit(solution)/shard_map/jit(_take)/gather | solution.py:44
  300.1 215.9 %gather_fusion = f32[65536,16]{1,0:T(8,128)} fusion(f32[511,16]{1,0:T(8,128)S(1)} %fusion.139, s32[65536]{0:T(1024)S(1)} %broadcast_clamp_fusion.1), kind=kCustom, calls=%fused_computation.clone | custom fusion | bytes 8650752 | tf_op jit(solution)/shard_map/jit(_take)/gather | solution.py:44
  516.1 20.3 %copy.84 = f32[1,256,256,16]{1,2,3,0:T(8,128)} copy(f32[1,256,256,16]{3,2,1,0:T(8,128)} %bitcast.191) | data formatting | bytes 8388608 | tf_op jit(solution)/shard_map/jit(_take)/gather | solution.py:44
  572.1 15.6 fusion.9
  587.8 6.7 fusion.3
  597.6 14.7 fusion.6
  612.4 4.2 fusion.2
  616.6 7.5 multiply_reduce_fusion
  629.9 3.6 fusion.21
  672.6 4.4 fusion.152
  677.1 10.1 convolution_add_fusion.1
  687.7 4.1 fusion.103
  691.8 9.8 convolution_add_fusion
  716.5 41.0 %all-reduce.4 = (f32[1024]{0:T(1024)S(1)}, f32[1024]{0:T(1024)S(1)}, f32[32,16]{0,1:T(8,128)}) all-reduce(f32[1024]{0:T(1024)S(1)} %add.436, f32[1024]{0:T(1024)S(1)} %add.441, f32[32,16]{0,1:T(8,128)S(1)} %fusion.84), channel_id=2, replica_groups=mesh['fsdp'=32] {'fsdp'}, use_global_device_ids=true, to_apply=%region_16.18.clone | all-reduce | flops 2560 | bytes 20480
  758.7 6.7 fusion.61
  765.5 6.0 fusion.60
  774.3 16.7 %reduce-scatter.7.cloned.1.call-done = f32[32,1024]{1,0:T(8,128)} async-done(((f32[1024,1024]{1,0:T(8,128)}), f32[32,1024]{1,0:T(8,128)}) %reduce-scatter.7.cloned.1.call-update) | async-done | bytes 131088 | tf_op jit(solution)/shard_map/reduce_scatter | solution.py:297
  790.9 139.7 %reduce-scatter.9.cloned.1.call-done = f32[32,1024]{1,0:T(8,128)} async-done(((f32[1024,1024]{1,0:T(8,128)}), f32[32,1024]{1,0:T(8,128)}) %reduce-scatter.9.cloned.1.call-update) | async-done | bytes 131088 | tf_op jit(solution)/shard_map/reduce_scatter | solution.py:297
  930.6 139.8 %reduce-scatter.11.cloned.1.call-done = f32[32,1024]{1,0:T(8,128)} async-done(((f32[1024,1024]{1,0:T(8,128)}), f32[32,1024]{1,0:T(8,128)}) %reduce-scatter.11.cloned.1.call-update) | async-done | bytes 131088 | tf_op jit(solution)/shard_map/reduce_scatter | solution.py:297
  1070.4 139.6 %reduce-scatter.13.cloned.1.call-done = f32[32,1024]{1,0:T(8,128)} async-done(((f32[1024,1024]{1,0:T(8,128)}), f32[32,1024]{1,0:T(8,128)}) %reduce-scatter.13.cloned.1.call-update) | async-done | bytes 131088 | tf_op jit(solution)/shard_map/reduce_scatter | solution.py:297
  1210.0 181.7 %reduce-scatter.15.cloned.1.call-done = f32[32,4096]{1,0:T(8,128)} async-done(((f32[1024,4096]{1,0:T(8,128)}), f32[32,4096]{1,0:T(8,128)}) %reduce-scatter.15.cloned.1.call-update) | async-done | bytes 524304 | tf_op jit(solution)/shard_map/reduce_scatter | solution.py:297
  1391.7 187.2 %reduce-scatter.17.cloned.1.call-done = f32[128,1024]{1,0:T(8,128)} async-done(((f32[4096,1024]{1,0:T(8,128)}), f32[128,1024]{1,0:T(8,128)}) %reduce-scatter.17.cloned.1.call-update) | async-done | bytes 524304 | tf_op jit(solution)/shard_map/reduce_scatter | solution.py:297
  (252 shorter events, 116.8 us)
Async XLA Ops:
  7.2 55.7 %copy-start = (f32[32,16]{0,1:T(8,128)S(1)}, f32[32,16]{0,1:T(8,128)}, u32[]{:S(2)}) copy-start(f32[32,16]{0,1:T(8,128)} %param.24) | copy-start | bytes 6148
  7.2 530.4 %all-gather.7.cloned.1.call-start = ((), (), s32[]{:S(2)}) async-start(), calls=%async_computation.6 | async-start | bytes 2162688 | tf_op jit(solution)/shard_map/all_gather | solution.py:254
  8.8 532.2 %all-gather.9.cloned.1.call-start = ((), (), s32[]{:S(2)}) async-start(), calls=%async_computation.7 | async-start | bytes 2162688 | tf_op jit(solution)/shard_map/all_gather | solution.py:252
  10.4 533.1 %all-gather.11.cloned.1.call-start = ((), (), s32[]{:S(2)}) async-start(), calls=%async_computation.8 | async-start | bytes 2162688 | tf_op jit(solution)/shard_map/all_gather | solution.py:253
  12.0 551.2 %all-gather.13.cloned.1.call-start = ((), (), s32[]{:S(2)}) async-start(), calls=%async_computation.9 | async-start | bytes 2162688 | tf_op jit(solution)/shard_map/all_gather | solution.py:255
  13.7 558.5 %all-gather.15.cloned.1.call-start = ((), (), s32[]{:S(2)}) async-start(), calls=%async_computation.10 | async-start | bytes 8650752 | tf_op jit(solution)/shard_map/all_gather | solution.py:259
  15.5 572.3 %all-gather.17.cloned.1.call-start = ((), (), s32[]{:S(2)}) async-start(), calls=%async_computation.11 | async-start | bytes 8650752 | tf_op jit(solution)/shard_map/all_gather | solution.py:260
  17.4 773.6 %reduce-scatter.7.cloned.1.call-start = ((), (), s32[]{:S(2)}) async-start(), calls=%async_computation.12 | async-start | bytes 4325376 | tf_op jit(solution)/shard_map/reduce_scatter | solution.py:297
  62.5 237.0 %copy-start.50 = (s32[256]{0:T(256)}, s32[256]{0:T(256)S(1)}, u32[]{:S(2)}) copy-start(s32[256]{0:T(256)S(1)} %get-tuple-element.38) | copy-start | bytes 3076
  62.5 237.0 %copy-start.52 = (s32[256]{0:T(256)}, s32[256]{0:T(256)S(1)}, u32[]{:S(2)}) copy-start(s32[256]{0:T(256)S(1)} %get-tuple-element.37) | copy-start | bytes 3076
  516.1 20.5 %copy-start.7 = (bf16[512,1024]{1,0:T(8,128)(2,1)S(1)}, bf16[512,1024]{1,0:T(8,128)(2,1)}, u32[]{:S(2)}) copy-start(bf16[512,1024]{1,0:T(8,128)(2,1)} %param.15) | copy-start | bytes 3145732
  516.1 20.7 %copy-start.58 = (s32[512]{0:T(512)S(1)}, s32[512]{0:T(512)}, u32[]{:S(2)}) copy-start(s32[512]{0:T(512)} %param.25) | copy-start | bytes 6148
  516.1 21.5 %copy-start.49 = (f32[1024]{0:T(1024)S(1)}, f32[1024]{0:T(1024)}, u32[]{:S(2)}) copy-start(f32[1024]{0:T(1024)} %convert_element_type.398) | copy-start | bytes 12292
  552.4 14.4 copy-start.32
  572.0 44.5 %copy-start.18 = (f32[256,1024]{1,0:T(8,128)}, f32[256,1024]{1,0:T(8,128)S(1)}, u32[]{:S(2)}) copy-start(f32[256,1024]{1,0:T(8,128)S(1)} %get-tuple-element.56) | copy-start | bytes 3145732
  595.0 17.4 %slice-start = ((s8[8388608]{0:T(1024)(128)(4,1)}), s8[4194304]{0:T(1024)(128)(4,1)S(1)}, s32[]{:S(2)}) async-start(s8[8388608]{0:T(1024)(128)(4,1)} %bitcast.227), calls=%async_computation.18 | async-start | bytes 8388608
  597.6 14.7 copy-start.37
  597.6 14.7 slice-start.1
  649.7 280.8 %reduce-scatter.9.cloned.1.call-start = ((), (), s32[]{:S(2)}) async-start(), calls=%async_computation.13 | async-start | bytes 4325376 | tf_op jit(solution)/shard_map/reduce_scatter | solution.py:297
  659.8 410.6 %reduce-scatter.11.cloned.1.call-start = ((), (), s32[]{:S(2)}) async-start(), calls=%async_computation.14 | async-start | bytes 4325376 | tf_op jit(solution)/shard_map/reduce_scatter | solution.py:297
  667.6 542.4 %reduce-scatter.13.cloned.1.call-start = ((), (), s32[]{:S(2)}) async-start(), calls=%async_computation.15 | async-start | bytes 4325376 | tf_op jit(solution)/shard_map/reduce_scatter | solution.py:297
  672.6 719.1 %reduce-scatter.15.cloned.1.call-start = ((), (), s32[]{:S(2)}) async-start(), calls=%async_computation.16 | async-start | bytes 17301504 | tf_op jit(solution)/shard_map/reduce_scatter | solution.py:297
  687.2 891.6 %reduce-scatter.17.cloned.1.call-start = ((), (), s32[]{:S(2)}) async-start(), calls=%async_computation.17 | async-start | bytes 17301504 | tf_op jit(solution)/shard_map/reduce_scatter | solution.py:297
  772.5 806.3 %copy-start.1 = (f32[32,16]{0,1:T(8,128)S(1)}, f32[32,16]{0,1:T(8,128)}, u32[]{:S(2)}) copy-start(f32[32,16]{0,1:T(8,128)} %param.24) | copy-start | bytes 6148
  (50 other events, 187.1 us)
Sparse Core Ops, SparseCore 0:
  11.5 59.4 all-gather.6
  74.4 55.2 all-gather.8
  133.1 55.2 all-gather.10
  191.6 55.2 all-gather.12
  249.6 76.3 all-gather.14
  328.7 76.0 all-gather.16
  649.9 141.0 reduce-scatter.6
  793.8 136.7 reduce-scatter.8
  933.4 136.9 reduce-scatter.10
  1073.1 136.8 reduce-scatter.12
  1212.9 178.7 reduce-scatter.14
  1394.4 184.3 reduce-scatter.16
where the time goes:
time: 1600 us; the launch traced here: 1590 us
  waiting for transfers between devices  805 us (50%)
  local copies, waits for them, and re-layouts  489 us (31%)
  matrix products  170 us (11%)
  blocking collectives  83.1 us (5%)
  other arithmetic  22.7 us (1%)
    reduce_scatter x6, waiting for transfers between devices, per_device(): lax.psum_scatter(totals, 'fsdp', scatter_dimension=0, tiled=True)  805 us
    gather x4, local copies, waits for them, and re-layouts, pair_layout(): biases = jnp.take(distance_table, relative + (length - 1), axis=0)  472 us
    unnamed x2, blocking collectives  83.1 us
  transfers between devices with their start and end apart: 12, of which 6 were waited for; matrix products, arithmetic and copies ran while one was open for 39% of the time, Pallas kernels for 0%

commit v1 on v0

v1 whole, which is shorter than its diff:
```python
import functools
import math

import jax
import jax.numpy as jnp
from jax import lax
from jax.experimental import pallas as pl
from jax.experimental.pallas import tpu as pltpu
from jax.sharding import PartitionSpec as P

AXIS = "fsdp"
HEADS = 16
HEAD = 64
NB = 32
SEQ = 256
SPAN = 2 * SEQ
LANES = 128
EPSILON = 1e-06
MASKED = -1000000000.0
LIMITS = (12, 16, 23, 32, 46, 64, 91)
HIGHEST = lax.Precision.HIGHEST
BF16 = jnp.bfloat16
F32 = jnp.float32
MIB = 1 << 20
VMEM_LIMIT = 56 * MIB
ANY = pl.BlockSpec(memory_space=pl.ANY)
VM = pl.BlockSpec(memory_space=pltpu.VMEM)


def bucket_of(relative):
    distance = jnp.abs(relative)
    counted = jnp.zeros_like(distance)
    for threshold in LIMITS:
        counted = counted + (distance >= threshold).astype(jnp.int32)
    inside = jnp.where(distance < 8, distance, 8 + counted)
    return inside + jnp.where(relative > 0, 16, 0).astype(jnp.int32)


def offset_lookup():
    k = lax.broadcasted_iota(jnp.int32, (8, SPAN, NB), 1)
    b = lax.broadcasted_iota(jnp.int32, (8, SPAN, NB), 0)
    c = lax.broadcasted_iota(jnp.int32, (8, SPAN, NB), 2)
    offset = k - b
    offset = jnp.where(offset >= SEQ, offset - SPAN, offset)
    return (bucket_of(offset) == c).astype(F32)


def bit_orders(n):
    if n == 32:
        x, y, z0, z1 = 1, 2, 3, 4
        return ((z0, z1, y, x, 0), (z1, x, z0, y, 0), (z1, y, x, z0, 0))
    high = list(range(1, n.bit_length() - 1))
    return tuple(tuple(high[k % len(high) :] + high[: k % len(high)] + [0]) for k in range(3))


def swap(array, bit, n):
    return lax.ppermute(array, AXIS, [(i, i ^ (1 << bit)) for i in range(n)])


def relative(bits, t):
    return sum(1 << b for k, b in enumerate(bits) if (t >> k) & 1)


def gather_stream(own, bits, n):
    have = own[None]
    for b in bits[:-2]:
        have = jnp.concatenate([have, swap(have, b, n)], axis=0)
    far = swap(have, bits[-2], n)
    return [have, far, swap(have, bits[-1], n), swap(far, bits[-1], n)]


def scatter_stream(send, keep, bits, n):
    total = keep.astype(F32) + swap(send, bits[-1], n).astype(F32)
    for b in reversed(bits[:-1]):
        half = total.shape[0] // 2
        given = swap(total[half:].astype(BF16), b, n)
        total = total[:half] + given.astype(F32)
    return total[0]


def sum_all(values, n):
    for b in range(n.bit_length() - 1):
        values = values + swap(values, b, n)
    return values


class Layout:
    def __init__(self, n, rows, cuts, orders):
        self.n, self.rows = n, rows
        self.cuts, self.orders = cuts, orders
        self.paired = n & (n - 1) == 0 and n >= 8 and rows % 16 == 0
        if not self.paired:
            self.cuts, self.orders = (cuts[-1],), (None,)

    def spans(self):
        return tuple(zip((0,) + tuple(self.cuts[:-1]), self.cuts))

    def gather(self, block):
        if not self.paired:
            return [lax.all_gather(block, AXIS, axis=0, tiled=True)]
        out = []
        for (lo, hi), bits in zip(self.spans(), self.orders):
            out += gather_stream(block[:, lo:hi], bits, self.n)
        return out

    def count(self):
        return 4 * len(self.cuts) if self.paired else 1

    def load(self, me, refs, full, sems):
        if not self.paired:
            copy = pltpu.make_async_copy(refs[0], full, sems.at[0])
            copy.start()
            return [copy.wait]
        waits = []
        for s, ((lo, hi), bits) in enumerate(zip(self.spans(), self.orders)):
            for q in range(4):
                ref = refs[4 * s + q]
                for j in range(self.n // 4):
                    row = pl.multiple_of((me ^ relative(bits, q * (self.n // 4) + j)) * self.rows, self.rows)
                    pltpu.make_async_copy(
                        ref.at[j], full.at[pl.ds(row, self.rows), lo:hi], sems.at[s]
                    ).start()
            view = full.at[:, lo:hi]
            waits.append(pltpu.make_async_copy(view, view, sems.at[s]).wait)
        return waits

    def out_shapes(self):
        if not self.paired:
            return [jax.ShapeDtypeStruct((self.n * self.rows, self.cuts[-1]), BF16)]
        half = self.n // 2
        return [
            jax.ShapeDtypeStruct((half, self.rows, hi - lo), BF16)
            for lo, hi in self.spans()
            for _ in range(2)
        ]

    def store(self, me, stage, refs, sems, s):
        if not self.paired:
            copy = pltpu.make_async_copy(stage, refs[0], sems.at[0])
            copy.start()
            return [copy.wait]
        lo, hi = self.spans()[s]
        half = self.n // 2
        waits = []
        for part in (1, 0):
            ref = refs[2 * s + 1 - part]
            for j in range(half):
                row = pl.multiple_of((me ^ relative(self.orders[s], part * half + j)) * self.rows, self.rows)
                pltpu.make_async_copy(
                    stage.at[pl.ds(row, self.rows), lo:hi], ref.at[j], sems.at[2 * s + part]
                ).start()
            waits.append(pltpu.make_async_copy(ref, ref, sems.at[2 * s + part]).wait)
        return waits

    def scatter(self, parts):
        if not self.paired:
            return lax.psum_scatter(parts[0].astype(F32), AXIS, scatter_dimension=0, tiled=True)
        pieces = [
            scatter_stream(parts[2 * s], parts[2 * s + 1], bits, self.n)
            for s, bits in enumerate(self.orders)
        ]
        return jnp.concatenate(pieces, axis=1)


def dot(a, b):
    return lax.dot_general(a, b, (((1,), (0,)), ((), ())), preferred_element_type=F32)


def dot_nt(a, b):
    return lax.dot_general(a, b, (((1,), (1,)), ((), ())), preferred_element_type=F32)


def dot_tn(a, b):
    return lax.dot_general(a, b, (((0,), (0,)), ((), ())), preferred_element_type=F32)


def row_scale(values):
    return lax.rsqrt(jnp.mean(values * values, axis=-1, keepdims=True) + EPSILON)


def toeplitz(base):
    return jnp.concatenate(
        [(pltpu.roll(base, 8 * a, 1) if a else base)[:, :SEQ] for a in range(SEQ // 8)], axis=0
    )


def diagonals(scores):
    total = None
    for a in range(SEQ // 8):
        rows = scores[8 * a : 8 * a + 8]
        rows = jnp.concatenate([rows, jnp.zeros((8, SPAN - SEQ), F32)], axis=1)
        if a:
            rows = pltpu.roll(rows, SPAN - 8 * a, 1)
        total = rows if total is None else total + rows
    return total


def transposed(values):
    return values.T


def copy_out(copies, sems, k, source, target):
    copy = pltpu.make_async_copy(source, target, sems.at[k])
    copy.start()
    copies.append(copy)


def attention_kernel(lay, seqs, width, *refs):
    m = lay.count()
    x_ref, segc_ref, segr_ref, base_ref = refs[:4]
    blocks = refs[4 : 4 + m]
    (wa_out, gain_ref, q_out, k_out, v_out, p_out, h1t_out, ct_out, x1_ref, h2_ref, h2t_ref) = refs[4 + m : 15 + m]
    wa, h1, q_s, k_s, v_s, c_s, p_s, h1t, ct, lsem, osem, psem = refs[15 + m :]
    me = lax.axis_index(AXIS)
    waits = lay.load(me, blocks, wa, lsem)
    for wait in waits:
        wait()
    copies = []
    copy_out(copies, osem, 0, wa, wa_out)
    gains = wa[:, 4 * width : 4 * width + LANES].astype(F32).T
    gain_ref[...] = gains[:8]
    x = x_ref[...].astype(F32)
    h1[...] = (x * row_scale(x) * gains[0:1]).astype(BF16)
    for k, (ref, out) in enumerate(((q_s, q_out), (k_s, k_out), (v_s, v_out))):
        for c in range(0, width, 512):
            ref[:, c : c + 512] = dot(h1[...], wa[:, k * width + c : k * width + c + 512]).astype(BF16)
        copy_out(copies, osem, 1 + k, ref, out)
    h1t[...] = transposed(h1[...])
    copy_out(copies, osem, 4, h1t, h1t_out)

    def pair(p, carry):
        lanes = pl.ds(pl.multiple_of(p * LANES, LANES), LANES)
        first = lax.broadcasted_iota(jnp.int32, (SEQ, LANES), 1) < HEAD
        biases = [toeplitz(base_ref[2 * p + o]) for o in range(2)]
        for s in range(seqs):
            rows = slice(s * SEQ, (s + 1) * SEQ)
            q2, k2, v2 = q_s[rows, lanes], k_s[rows, lanes], v_s[rows, lanes]
            allowed = segc_ref[rows, :] == segr_ref[s : s + 1, :]
            made = []
            for o in range(2):
                mine = jnp.where(first == (o == 0), q2, jnp.zeros_like(q2))
                scores = jnp.where(allowed, dot_nt(mine, k2) + biases[o], MASKED)
                exponent = jnp.exp(scores - jnp.max(scores, axis=-1, keepdims=True))
                prob = exponent * (1.0 / jnp.sum(exponent, axis=-1, keepdims=True))
                p_s[s, 2 * p + o] = prob
                made.append(dot(prob.astype(BF16), v2))
            c_s[rows, lanes] = jnp.where(first, made[0], made[1]).astype(BF16)
            pltpu.make_async_copy(p_s.at[s, pl.ds(2 * p, 2)], p_out.at[s, pl.ds(2 * p, 2)], psem).start()
        return carry

    lax.fori_loop(0, HEADS // 2, pair, 0)
    ct[...] = transposed(c_s[...])
    copy_out(copies, osem, 5, ct, ct_out)
    for c in range(0, width, 512):
        x1_ref[:, c : c + 512] = x_ref[:, c : c + 512].astype(F32) + dot(
            c_s[...], wa[:, 3 * width + c : 3 * width + c + 512]
        )
    x1 = x1_ref[...]
    h2 = (x1 * row_scale(x1) * gains[1:2]).astype(BF16)
    h2_ref[...] = h2
    h2t_ref[...] = transposed(h2)
    for copy in copies:
        copy.wait()
    pltpu.make_async_copy(p_s, p_out, psem).wait()


def attention_forward(lay, x, segments, base, blocks):
    tokens, width = x.shape
    seqs = tokens // SEQ
    wide = lay.cuts[-1]
    sds = jax.ShapeDtypeStruct
    shapes = [
        sds((width, wide), BF16),
        sds((8, width), F32),
        sds((tokens, width), BF16),
        sds((tokens, width), BF16),
        sds((tokens, width), BF16),
        sds((seqs, HEADS, SEQ, SEQ), F32),
        sds((width, tokens), BF16),
        sds((width, tokens), BF16),
        sds((tokens, width), F32),
        sds((tokens, width), BF16),
        sds((width, tokens), BF16),
    ]
    flops = 2 * tokens * width * 4 * width + 4 * tokens * SEQ * width
    return pl.pallas_call(
        functools.partial(attention_kernel, lay, seqs, width),
        out_shape=shapes,
        in_specs=[VM] * 4 + [ANY] * len(blocks),
        out_specs=[ANY, VM] + [ANY] * 6 + [VM] * 3,
        scratch_shapes=[
            pltpu.VMEM((width, wide), BF16),
            pltpu.VMEM((tokens, width), BF16),
            pltpu.VMEM((tokens, width), BF16),
            pltpu.VMEM((tokens, width), BF16),
            pltpu.VMEM((tokens, width), BF16),
            pltpu.VMEM((tokens, width), BF16),
            pltpu.VMEM((seqs, HEADS, SEQ, SEQ), F32),
            pltpu.VMEM((width, tokens), BF16),
            pltpu.VMEM((width, tokens), BF16),
            pltpu.SemaphoreType.DMA((max(1, len(lay.cuts)),)),
            pltpu.SemaphoreType.DMA((6,)),
            pltpu.SemaphoreType.DMA,
        ],
        compiler_params=pltpu.CompilerParams(vmem_limit_bytes=VMEM_LIMIT),
        cost_estimate=pl.CostEstimate(flops=flops, transcendentals=tokens * SEQ * HEADS, bytes_accessed=40 * MIB),
        name="attention_forward",
    )(x, segments.reshape(tokens, 1), segments.reshape(seqs, SEQ), base, *blocks)


def inner_kernel(lay, lay_out, chunk, *refs):
    m, k = lay.count(), len(lay_out.out_shapes())
    h2_ref, e_ref = refs[:2]
    blocks = refs[2 : 2 + m]
    z_out, g_out = refs[2 + m : 4 + m]
    grads = refs[4 + m : 4 + m + k]
    wi, z_s, g_s, stage, lsem, osem, gsem = refs[4 + m + k :]
    me = lax.axis_index(AXIS)
    for wait in lay.load(me, blocks, wi, lsem):
        wait()
    hidden = wi.shape[1]

    def step(c, carry):
        cols = pl.ds(pl.multiple_of(c * chunk, chunk), chunk)
        u = dot(h2_ref[...], wi[:, cols])
        cdf = 0.5 * (1.0 + lax.erf(u * (1.0 / math.sqrt(2.0))))
        z = (u * cdf).astype(BF16)
        z_s[:, cols] = z
        g_s[:, cols] = cdf + u * jnp.exp(-0.5 * u * u) * (1.0 / math.sqrt(2.0 * math.pi))
        stage[cols, :] = dot(transposed(z), e_ref[...]).astype(BF16)
        pltpu.make_async_copy(z_s.at[:, cols], z_out.at[:, cols], osem.at[0]).start()
        pltpu.make_async_copy(g_s.at[:, cols], g_out.at[:, cols], osem.at[1]).start()
        return carry

    lax.fori_loop(0, hidden // chunk, step, 0)
    waits = []
    for s in range(len(lay_out.cuts)):
        waits += lay_out.store(me, stage, grads, gsem, s)
    pltpu.make_async_copy(z_s, z_out, osem.at[0]).wait()
    pltpu.make_async_copy(g_s, g_out, osem.at[1]).wait()
    for wait in waits:
        wait()


def inner_forward(lay, lay_out, h2, cotangent, blocks, hidden):
    tokens, width = h2.shape
    sds = jax.ShapeDtypeStruct
    grads = lay_out.out_shapes()
    return pl.pallas_call(
        functools.partial(inner_kernel, lay, lay_out, 512),
        out_shape=[sds((tokens, hidden), BF16), sds((tokens, hidden), F32)] + grads,
        in_specs=[VM] * 2 + [ANY] * len(blocks),
        out_specs=[ANY] * (2 + len(grads)),
        scratch_shapes=[
            pltpu.VMEM((width, hidden), BF16),
            pltpu.VMEM((tokens, hidden), BF16),
            pltpu.VMEM((tokens, hidden), F32),
            pltpu.VMEM((hidden, width), BF16),
            pltpu.SemaphoreType.DMA((max(1, len(lay.cuts)),)),
            pltpu.SemaphoreType.DMA((2,)),
            pltpu.SemaphoreType.DMA((2 * len(lay_out.cuts),)),
        ],
        compiler_params=pltpu.CompilerParams(vmem_limit_bytes=VMEM_LIMIT),
        cost_estimate=pl.CostEstimate(
            flops=4 * tokens * width * hidden, transcendentals=2 * tokens * hidden, bytes_accessed=32 * MIB
        ),
        name="feedforward_inner",
    )(h2, cotangent, *blocks)


def outer_kernel(lay_i, lay_f, lay_g, lay_o, chunk, *refs):
    mi, mf = lay_i.count(), lay_f.count()
    kg, ko = len(lay_g.out_shapes()), len(lay_o.out_shapes())
    e_ref, x1_ref, h2t_ref, gain_ref, g_in, ct_in = refs[:6]
    at = 6
    inner, outer = refs[at : at + mi], refs[at + mi : at + mi + mf]
    at += mi + mf
    dx1_ref, da_ref, dgain_ref = refs[at : at + 3]
    grads, grads_o = refs[at + 3 : at + 3 + kg], refs[at + 3 + kg : at + 3 + kg + ko]
    wi, wf, g_s, ct, stage, stage_o, lsem, isem, gsem, osem = refs[at + 3 + kg + ko :]
    me = lax.axis_index(AXIS)
    hidden = wi.shape[1]
    waits = lay_f.load(me, outer, wf, lsem.at[0]) + lay_i.load(me, inner, wi, lsem.at[1])
    steps = hidden // chunk
    for c in range(steps):
        cols = slice(c * chunk, (c + 1) * chunk)
        pltpu.make_async_copy(g_in.at[:, cols], g_s.at[:, cols], isem.at[c]).start()
    ct_copy = pltpu.make_async_copy(ct_in, ct, isem.at[steps])
    ct_copy.start()
    for wait in waits:
        wait()
    e = e_ref[...]
    dh2 = None
    done = []
    sent = 0
    for c in range(steps):
        cols = slice(c * chunk, (c + 1) * chunk)
        pltpu.make_async_copy(g_in.at[:, cols], g_s.at[:, cols], isem.at[c]).wait()
        du = (dot_nt(e, wf[cols, :]) * g_s[:, cols]).astype(BF16)
        stage[:, cols] = dot(h2t_ref[...], du).astype(BF16)
        part = dot_nt(du, wi[:, cols])
        if dh2 is None:
            dx1_ref[...] = part
            dh2 = True
        else:
            dx1_ref[...] += part
        if lay_g.paired:
            while sent < len(lay_g.cuts) and lay_g.cuts[sent] <= (c + 1) * chunk:
                done += lay_g.store(me, stage, grads, gsem, sent)
                sent += 1
    if not lay_g.paired:
        done += lay_g.store(me, stage, grads, gsem, 0)
    dh2 = dx1_ref[...]
    x1 = x1_ref[...]
    gain = gain_ref[1:2, :]
    scale = row_scale(x1)
    dgain_ref[...] = jnp.broadcast_to(jnp.sum(dh2 * (x1 * scale), axis=0, keepdims=True), dgain_ref.shape)
    mean = jnp.mean(x1 * gain * dh2, axis=-1, keepdims=True)
    dx1 = e.astype(F32) + scale * gain * dh2 - x1 * (scale * scale * scale) * mean
    dx1_ref[...] = dx1
    da = dx1.astype(BF16)
    da_ref[...] = da
    ct_copy.wait()
    stage_o[...] = dot(ct[...], da).astype(BF16)
    for s in range(len(lay_o.cuts)):
        done += lay_o.store(me, stage_o, grads_o, osem, s)
    for wait in done:
        wait()


def outer_backward(lay_i, lay_f, lay_g, lay_o, cotangent, x1, h2t, gain, g, ct, inner, outer, hidden):
    tokens, width = x1.shape
    chunk = 512
    sds = jax.ShapeDtypeStruct
    grads, grads_o = lay_g.out_shapes(), lay_o.out_shapes()
    return pl.pallas_call(
        functools.partial(outer_kernel, lay_i, lay_f, lay_g, lay_o, chunk),
        out_shape=[sds((tokens, width), F32), sds((tokens, width), BF16), sds((8, width), F32)] + grads + grads_o,
        in_specs=[VM] * 4 + [ANY] * (2 + len(inner) + len(outer)),
        out_specs=[VM] * 3 + [ANY] * (len(grads) + len(grads_o)),
        scratch_shapes=[
            pltpu.VMEM((width, hidden), BF16),
            pltpu.VMEM((hidden, width), BF16),
            pltpu.VMEM((tokens, hidden), F32),
            pltpu.VMEM((width, tokens), BF16),
            pltpu.VMEM((width, hidden), BF16),
            pltpu.VMEM((width, width), BF16),
            pltpu.SemaphoreType.DMA((2, 4)),
            pltpu.SemaphoreType.DMA((hidden // chunk + 1,)),
            pltpu.SemaphoreType.DMA((8,)),
            pltpu.SemaphoreType.DMA((8,)),
        ],
        compiler_params=pltpu.CompilerParams(vmem_limit_bytes=VMEM_LIMIT),
        cost_estimate=pl.CostEstimate(
            flops=6 * tokens * width * hidden + 2 * tokens * width * width,
            transcendentals=tokens,
            bytes_accessed=48 * MIB,
        ),
        name="feedforward_outer",
    )(cotangent, x1, h2t, gain, g, ct, *inner, *outer)


def scores_kernel(lay, seqs, width, *refs):
    k = len(lay.out_shapes())
    da_ref, q_ref, k_ref, v_ref, h1t_ref, wa_in, p_in = refs[:7]
    dq_ref, dk_ref, dv_ref, table_ref = refs[7:11]
    grads = refs[11 : 11 + k]
    wo, p_s, dc, stage, isem, psem, gsem = refs[11 + k :]
    me = lax.axis_index(AXIS)
    wo_copy = pltpu.make_async_copy(wa_in.at[:, 3 * width : 4 * width], wo, isem)
    wo_copy.start()
    for p in range(HEADS // 2):
        pltpu.make_async_copy(p_in.at[:, 2 * p : 2 * p + 2], p_s.at[:, 2 * p : 2 * p + 2], psem.at[p]).start()
    wo_copy.wait()
    for c in range(0, width, 512):
        dc[:, c : c + 512] = dot_nt(da_ref[...], wo[c : c + 512, :]).astype(BF16)

    def pair(p, carry):
        lanes = pl.ds(pl.multiple_of(p * LANES, LANES), LANES)
        heads = pl.ds(2 * p, 2)
        first = lax.broadcasted_iota(jnp.int32, (SEQ, LANES), 1) < HEAD
        pltpu.make_async_copy(p_in.at[:, heads], p_s.at[:, heads], psem.at[p]).wait()
        for o in range(2):
            total = None
            for s in range(seqs):
                rows = slice(s * SEQ, (s + 1) * SEQ)
                dc2, q2, k2, v2 = dc[rows, lanes], q_ref[rows, lanes], k_ref[rows, lanes], v_ref[rows, lanes]
                prob = p_s[s, 2 * p + o]
                mine = jnp.where(first == (o == 0), dc2, jnp.zeros_like(dc2))
                dprob = dot_nt(mine, v2)
                inner = jnp.sum(prob * dprob, axis=-1, keepdims=True)
                ds = (prob * (dprob - inner)).astype(BF16)
                wide = ds.astype(F32)
                total = wide if total is None else total + wide
                dv = dot(transposed(prob.astype(BF16)), dc2).astype(BF16)
                dq = dot(ds, k2).astype(BF16)
                dk = dot(transposed(ds), q2).astype(BF16)
                for ref, value in ((dv_ref, dv), (dq_ref, dq), (dk_ref, dk)):
                    if o == 0:
                        ref[rows, lanes] = value
                    else:
                        ref[rows, lanes] = jnp.where(first, ref[rows, lanes], value)
            table_ref[2 * p + o] = diagonals(total)
        return carry

    lax.fori_loop(0, HEADS // 2, pair, 0)
    for j, ref in enumerate((dq_ref, dk_ref, dv_ref)):
        for c in range(0, width, 512):
            stage[:, j * width + c : j * width + c + 512] = dot(h1t_ref[...], ref[:, c : c + 512]).astype(BF16)
    waits = []
    for s in range(len(lay.cuts)):
        waits += lay.store(me, stage, grads, gsem, s)
    for wait in waits:
        wait()


def scores_backward(lay, da, q, k, v, h1t, wa, p):
    tokens, width = da.shape
    seqs = tokens // SEQ
    sds = jax.ShapeDtypeStruct
    grads = lay.out_shapes()
    return pl.pallas_call(
        functools.partial(scores_kernel, lay, seqs, width),
        out_shape=[sds((tokens, width), BF16)] * 3 + [sds((HEADS, 8, SPAN), F32)] + grads,
        in_specs=[VM] * 5 + [ANY] * 2,
        out_specs=[VM] * 4 + [ANY] * len(grads),
        scratch_shapes=[
            pltpu.VMEM((width, width), BF16),
            pltpu.VMEM((seqs, HEADS, SEQ, SEQ), F32),
            pltpu.VMEM((tokens, width), BF16),
            pltpu.VMEM((width, 3 * width), BF16),
            pltpu.SemaphoreType.DMA,
            pltpu.SemaphoreType.DMA((HEADS // 2,)),
            pltpu.SemaphoreType.DMA((8,)),
        ],
        compiler_params=pltpu.CompilerParams(vmem_limit_bytes=VMEM_LIMIT),
        cost_estimate=pl.CostEstimate(
            flops=2 * tokens * width * 4 * width + 8 * tokens * SEQ * width,
            transcendentals=0,
            bytes_accessed=32 * MIB,
        ),
        name="attention_backward",
    )(da, q, k, v, h1t, wa, p)


def inputs_kernel(width, *refs):
    x_ref, dx1_ref, gain_ref, dq_ref, dk_ref, dv_ref, wa_in, dx_ref, dgain_ref, wa, dh, sem = refs
    copies = []
    for j in range(3):
        cols = slice(j * width, (j + 1) * width)
        copy_out(copies, sem, j, wa_in.at[:, cols], wa.at[:, cols])
    for j, ref in enumerate((dq_ref, dk_ref, dv_ref)):
        copies[j].wait()
        for c in range(0, width, 512):
            part = dot_nt(ref[...], wa[c : c + 512, j * width : (j + 1) * width])
            if j:
                dh[:, c : c + 512] += part
            else:
                dh[:, c : c + 512] = part
    x = x_ref[...].astype(F32)
    gain = gain_ref[0:1, :]
    scale = row_scale(x)
    dh1 = dh[...]
    dgain_ref[...] = jnp.broadcast_to(jnp.sum(dh1 * (x * scale), axis=0, keepdims=True), dgain_ref.shape)
    mean = jnp.mean(x * gain * dh1, axis=-1, keepdims=True)
    dx_ref[...] = (dx1_ref[...] + scale * gain * dh1 - x * (scale * scale * scale) * mean).astype(BF16)


def inputs_backward(x, dx1, gain, dq, dk, dv, wa):
    tokens, width = x.shape
    sds = jax.ShapeDtypeStruct
    return pl.pallas_call(
        functools.partial(inputs_kernel, width),
        out_shape=[sds((tokens, width), BF16), sds((8, width), F32)],
        in_specs=[VM] * 6 + [ANY],
        out_specs=[VM] * 2,
        scratch_shapes=[
            pltpu.VMEM((width, 3 * width), BF16),
            pltpu.VMEM((tokens, width), F32),
            pltpu.SemaphoreType.DMA((3,)),
        ],
        compiler_params=pltpu.CompilerParams(vmem_limit_bytes=VMEM_LIMIT),
        cost_estimate=pl.CostEstimate(
            flops=6 * tokens * width * width, transcendentals=tokens, bytes_accessed=16 * MIB
        ),
        name="inputs_backward",
    )(x, dx1, gain, dq, dk, dv, wa)


def output_kernel(lay, *refs):
    m = lay.count()
    x1_ref, z_ref = refs[:2]
    blocks = refs[2 : 2 + m]
    out_ref, wf, sem = refs[2 + m :]
    me = lax.axis_index(AXIS)
    for wait in lay.load(me, blocks, wf, sem):
        wait()
    width = wf.shape[1]
    for c in range(0, width, 512):
        cols = slice(c, c + 512)
        out_ref[:, cols] = (x1_ref[:, cols] + dot(z_ref[...], wf[:, cols])).astype(BF16)


def layer_output(lay, x1, z, blocks):
    tokens, width = x1.shape
    hidden = z.shape[1]
    return pl.pallas_call(
        functools.partial(output_kernel, lay),
        out_shape=jax.ShapeDtypeStruct((tokens, width), BF16),
        in_specs=[VM] * 2 + [ANY] * len(blocks),
        out_specs=VM,
        scratch_shapes=[
            pltpu.VMEM((hidden, width), BF16),
            pltpu.SemaphoreType.DMA((max(1, len(lay.cuts)),)),
        ],
        compiler_params=pltpu.CompilerParams(vmem_limit_bytes=VMEM_LIMIT),
        cost_estimate=pl.CostEstimate(
            flops=2 * tokens * width * hidden, transcendentals=0, bytes_accessed=16 * MIB
        ),
        name="layer_output",
    )(x1, z, *blocks)


def per_device(
    n,
    tokens,
    attention_gain,
    query_weight,
    key_weight,
    value_weight,
    output_weight,
    feedforward_gain,
    inner_weight,
    outer_weight,
    bias_table,
    segment_ids,
    positions,
    cotangent,
):
    del positions
    width = tokens.shape[1]
    hidden = inner_weight.shape[1]
    rows = query_weight.shape[0]
    first, second, third = bit_orders(n)
    lay_a = Layout(n, rows, (1536, 3072, 4 * width + LANES), (first, second, third))
    lay_i = Layout(n, rows, (hidden // 2, hidden), (first, second))
    lay_f = Layout(n, outer_weight.shape[0], (width // 2, width), (third, first))
    lay_df = Layout(n, outer_weight.shape[0], (width // 2, width), (first, second))
    lay_di = Layout(n, rows, (hidden // 2, hidden), (third, second))
    lay_do = Layout(n, rows, (width,), (first,))
    lay_da = Layout(n, rows, (width, 2 * width, 3 * width), (first, second, third))

    gains = jnp.pad(jnp.stack([attention_gain, feedforward_gain], axis=1), ((0, 0), (0, LANES - 2)))
    block_a = jnp.concatenate(
        [query_weight, key_weight, value_weight, output_weight, gains], axis=1
    ).astype(BF16)
    sources_a = lay_a.gather(block_a)
    sources_i = lay_i.gather(inner_weight.astype(BF16))
    sources_f = lay_f.gather(outer_weight.astype(BF16))
    lookup = offset_lookup()
    base = jnp.einsum("bkc,ch->hbk", lookup, bias_table, precision=HIGHEST)

    wa, gain, q, k, v, p, h1t, ct, x1, h2, h2t = attention_forward(lay_a, tokens, segment_ids, base, sources_a)
    z, g, *parts_f = inner_forward(lay_i, lay_df, h2, cotangent, sources_i, hidden)
    outer_gradient = lay_df.scatter(parts_f)
    dx1, da, dgain2, *parts = outer_backward(
        lay_i, lay_f, lay_di, lay_do, cotangent, x1, h2t, gain, g, ct, sources_i, sources_f, hidden
    )
    split = len(lay_di.out_shapes())
    inner_gradient = lay_di.scatter(parts[:split])
    output_gradient = lay_do.scatter(parts[split:])
    dq, dk, dv, diagonal, *parts_a = scores_backward(lay_da, da, q, k, v, h1t, wa, p)
    projections = lay_da.scatter(parts_a)
    tokens_gradient, dgain1 = inputs_backward(tokens, dx1, gain, dq, dk, dv, wa)
    table = jnp.einsum("hbk,bkc->ch", diagonal, lookup, precision=HIGHEST)
    small = jnp.concatenate([dgain1[0], dgain2[0], table.reshape(-1)])
    small = sum_all(small, n) if n & (n - 1) == 0 else lax.psum(small, AXIS)
    start = lax.axis_index(AXIS) * rows
    result = layer_output(lay_f, x1, z, sources_f)
    return (
        result,
        tokens_gradient,
        lax.dynamic_slice(small, (start,), (rows,)),
        projections[:, :width],
        projections[:, width : 2 * width],
        projections[:, 2 * width :],
        output_gradient,
        lax.dynamic_slice(small, (width + start,), (rows,)),
        inner_gradient,
        outer_gradient,
        small[2 * width :].reshape(NB, HEADS),
    )


def solution(mesh):
    n = mesh.shape[AXIS]
    matrix, vector = P(AXIS, None), P(AXIS)
    return jax.shard_map(
        functools.partial(per_device, n),
        mesh=mesh,
        in_specs=(
            matrix,
            vector,
            matrix,
            matrix,
            matrix,
            matrix,
            vector,
            matrix,
            matrix,
            P(),
            vector,
            vector,
            matrix,
        ),
        out_specs=(
            matrix,
            matrix,
            vector,
            matrix,
            matrix,
            matrix,
            matrix,
            vector,
            matrix,
            matrix,
            P(),
        ),
        check_vma=False,
    )
```

time: 1600 us -> 481 us (0.30)
  waiting for transfers between devices: 805 us -> 228 us
  local copies, waits for them, and re-layouts: 489 us -> 13.7 us
  matrix products: 170 us -> 0.92 us
  Pallas kernels: 0 us -> 130 us
  blocking collectives: 83.1 us -> 0 us
  starting transfers between devices: 1.12 us -> 75.2 us
    reduce_scatter x6 -> x0, waiting for transfers between devices: 805 us -> none  [per_device(): lax.psum_scatter(totals, 'fsdp', scatter_dimension=0, tiled=True)]
    gather x4 -> x0, local copies, waits for them, and re-layouts: 472 us -> none  [pair_layout(): biases = jnp.take(distance_table, relative + (length - 1), axis=0)]
    ppermute x0 -> x87, waiting for transfers between devices: none -> 228 us  [swap(): return lax.ppermute(array, AXIS, [(i, i ^ 1 << bit) for i in range(n)])]
    dot_general x51 -> x2, matrix products: 170 us -> 0.92 us  [the longest x1 0.55 us: per_device(): table = jnp.einsum('hbk,bkc->ch', diagonal, lookup, precision=HIGHEST)]
    pallas_call x0 -> x6, Pallas kernels: none -> 130 us  [the longest x1 31.5 us: outer_backward(): pl.pallas_call(functools.partial(outer_kernel, lay_i, lay_f, lay_g, lay_o...]
    unnamed x2 -> x0, blocking collectives: 83.1 us -> none
    ppermute x0 -> x87, starting transfers between devices: none -> 75.2 us  [swap(): return lax.ppermute(array, AXIS, [(i, i ^ 1 << bit) for i in range(n)])]
  transfers between devices with their start and end apart: 12 -> 87, of which waited for: 6 -> 43; matrix products, arithmetic and copies ran while one was open for 39% -> 6% of each run, Pallas kernels for 0% -> 21%
where the time goes in v1:
time: 481 us; the launch traced here: 474 us
  waiting for transfers between devices  228 us (47%)
  Pallas kernels  130 us (27%)
  starting transfers between devices  75.2 us (16%)
  other arithmetic  24.1 us (5%)
  local copies, waits for them, and re-layouts  13.7 us (3%)
    ppermute x87, waiting for transfers between devices, swap(): return lax.ppermute(array, AXIS, [(i, i ^ 1 << bit) for i in range(n)])  228 us
    ppermute x87, starting transfers between devices, swap(): return lax.ppermute(array, AXIS, [(i, i ^ 1 << bit) for i in range(n)])  75.2 us
    pallas_call x1, Pallas kernels, outer_backward(): pl.pallas_call(functools.partial(outer_kernel, lay_i, lay_f, lay_g, lay_o...  31.5 us
    pallas_call x1, Pallas kernels, attention_forward(): pl.pallas_call(functools.partial(attention_kernel, lay, seqs, width), out...  27.9 us
    pallas_call x1, Pallas kernels, scores_backward(): pl.pallas_call(functools.partial(scores_kernel, lay, seqs, width), out_sh...  27.1 us
    pallas_call x1, Pallas kernels, inner_forward(): pl.pallas_call(functools.partial(inner_kernel, lay, lay_out, 512), out_sh...  21.4 us
    pallas_call x1, Pallas kernels, layer_output(): pl.pallas_call(functools.partial(output_kernel, lay), out_shape=jax.Shape...  11.8 us
    add x8, other arithmetic, scatter_stream(): total = keep.astype(F32) + swap(send, bits[-1], n).astype(F32)  9.74 us
  transfers between devices with their start and end apart: 87, of which 43 were waited for; matrix products, arithmetic and copies ran while one was open for 6% of the time, Pallas kernels for 21%

profile of v1, /device:TPU:0, one launch (start us, length us, event | category | flops | bytes accessed | tf_op | source)
XLA Modules:
  0.0 474.1 jit_solution(13885126038165624500)
XLA Ops:
  36.1 6.4 %collective-permute-done.1 = bf16[2,32,1536]{2,1,0:T(8,128)(2,1)S(1)} collective-permute-done((bf16[2,32,1536]{2,1,0:T(8,128)(2,1)S(1)}, bf16[2,32,1536]{2,1,0:T(8,128)(2,1)S(1)}, u32[]{:S(2)}, u32[]{:S(2)}) %collective-permute-start.1) | collective-permute-done | bytes 196640 | tf_op jit(solution)/shard_map/ppermute | solution.py:57
  48.1 6.3 %collective-permute-start.8 = (bf16[4,32,1536]{2,1,0:T(8,128)(2,1)S(1)}, bf16[4,32,1536]{2,1,0:T(8,128)(2,1)S(1)}, u32[]{:S(2)}, u32[]{:S(2)}) collective-permute-start(bf16[4,32,1536]{2,1,0:T(8,128)(2,1)S(1)} %pad_maximum_fusion.14), channel_id=1, source_target_pairs={{0,8},{1,9},{2,10},{3,11},{4,12},{5,13},{6,14},{7,15},{8,0},{9,1},... | collective-permute-start | bytes 1179656 | tf_op jit(solution)/shard_map/ppermute | solution.py:57
  67.3 10.5 %collective-permute-done.20 = bf16[4,32,2048]{2,1,0:T(8,128)(2,1)S(1)} collective-permute-done((bf16[4,32,2048]{2,1,0:T(8,128)(2,1)S(1)}, bf16[4,32,2048]{2,1,0:T(8,128)(2,1)S(1)}, u32[]{:S(2)}, u32[]{:S(2)}) %collective-permute-start.20) | collective-permute-done | bytes 524320 | tf_op jit(solution)/shard_map/ppermute | solution.py:57
  81.1 5.9 %collective-permute-done.38 = bf16[4,128,512]{2,1,0:T(8,128)(2,1)S(1)} collective-permute-done((bf16[4,128,512]{2,1,0:T(8,128)(2,1)S(1)}, bf16[4,128,512]{2,1,0:T(8,128)(2,1)S(1)}, u32[]{:S(2)}, u32[]{:S(2)}) %collective-permute-start.38) | collective-permute-done | bytes 524320 | tf_op jit(solution)/shard_map/ppermute | solution.py:57
  89.9 11.1 %collective-permute-done.9.refs_9_ = bf16[8,32,1536]{2,1,0:T(8,128)(2,1)} collective-permute-done((bf16[8,32,1536]{2,1,0:T(8,128)(2,1)S(1)}, bf16[8,32,1536]{2,1,0:T(8,128)(2,1)}, u32[]{:S(2)}, u32[]{:S(2)}) %collective-permute-start.9) | collective-permute-done | bytes 786464 | tf_op jit(solution)/shard_map/ppermute | solution.py:57
  106.9 14.8 %collective-permute-done.21.refs_3_.refs_7_ = bf16[8,32,2048]{2,1,0:T(8,128)(2,1)} collective-permute-done((bf16[8,32,2048]{2,1,0:T(8,128)(2,1)S(1)}, bf16[8,32,2048]{2,1,0:T(8,128)(2,1)}, u32[]{:S(2)}, u32[]{:S(2)}) %collective-permute-start.21) | collective-permute-done | bytes 1048608 | tf_op jit(solution)/shard_map/ppermute | solution.py:57
  133.1 13.2 %collective-permute-done.39.refs_7_.refs_19_ = bf16[8,128,512]{2,1,0:T(8,128)(2,1)} collective-permute-done((bf16[8,128,512]{2,1,0:T(8,128)(2,1)S(1)}, bf16[8,128,512]{2,1,0:T(8,128)(2,1)}, u32[]{:S(2)}, u32[]{:S(2)}) %collective-permute-start.39) | collective-permute-done | bytes 1048608 | tf_op jit(solution)/shard_map/ppermute | solution.py:57
  147.4 27.9 %attention_forward.1 = (bf16[1024,4224]{1,0:T(8,128)(2,1)}, f32[8,1024]{1,0:T(8,128)}, bf16[512,1024]{1,0:T(8,128)(2,1)}, bf16[512,1024]{1,0:T(8,128)(2,1)}, bf1...) custom-call(bf16[512,1024]{1,0:T(8,128)(2,1)} %refs_0_.5, ...), custom_call_target="tpu_custom_call" | custom-call | flops 4831838208 | bytes 41943040 | tf_op jit(solution)/shard_map/attention_forward/pallas_call | solution.py:286
  175.3 21.4 %feedforward_inner.1 = (bf16[512,4096]{1,0:T(8,128)(2,1)}, f32[512,4096]{1,0:T(8,128)}, bf16[16,128,512]{2,1,0:T(8,128)(2,1)}, bf16[16,128,512]{2,1,0:T(8,128)(2...) custom-call(bf16[512,1024]{1,0:T(8,128)(2,1)} %get-tuple-element.50.refs_0_, ...), custom_call_target="tpu_custom_call" | custom-call | flops 8589934592 | bytes 33554432 | tf_op jit(solution)/shard_map/feedforward_inner/pallas_call | solution.py:349
  198.7 31.5 %feedforward_outer.1 = (f32[512,1024]{1,0:T(8,128)}, bf16[512,1024]{1,0:T(8,128)(2,1)}, f32[8,1024]{1,0:T(8,128)}, bf16[16,32,2048]{2,1,0:T(8,128)(2,1)}, bf16[1...) custom-call(bf16[512,1024]{1,0:T(8,128)(2,1)} %refs_0_.4, ...), custom_call_target="tpu_custom_call" | custom-call | flops 13958643712 | bytes 50331648 | tf_op jit(solution)/shard_map/feedforward_outer/pallas_call | solution.py:436
  230.4 27.1 %attention_backward.1 = (bf16[512,1024]{1,0:T(8,128)(2,1)}, bf16[512,1024]{1,0:T(8,128)(2,1)}, bf16[512,1024]{1,0:T(8,128)(2,1)}, f32[16,8,512]{2,1,0:T(8,128)},...) custom-call(bf16[512,1024]{1,0:T(8,128)(2,1)} %get-tuple-element.57., ...), custom_call_target="tpu_custom_call" | custom-call | flops 5368709120 | bytes 33554432 | tf_op jit(solution)/shard_map/attention_backward/pallas_call | solution.py:522
  257.6 9.7 %inputs_backward.1 = (bf16[512,1024]{1,0:T(8,128)(2,1)}, f32[8,1024]{1,0:T(8,128)}) custom-call(bf16[512,1024]{1,0:T(8,128)(2,1)} %refs_0_.5, f32[512,1024]{1,0:T(8,128)} %get-tuple-element.56.refs_1_, f32[8,1024]{1,0:T(8,128)} %get-tuple-element.53.refs_3_.refs_2_, bf16[512,1024]{1,0:T(8,128)(2,1)} %get-tuple-element.64.refs_3_, ...), custom_call_target="tpu_custom_call" | custom-call | flops 3221225472 | bytes 16777216 | tf_op jit(solution)/shard_map/inputs_backward/pallas_call | solution.py:572
  285.4 11.8 %layer_output.1 = bf16[512,1024]{1,0:T(8,128)(2,1)} custom-call(f32[512,1024]{1,0:T(8,128)} %get-tuple-element.49.refs_0_.refs_1_, bf16[512,4096]{1,0:T(8,128)(2,1)} %get-tuple-element.51.refs_1_, bf16[8,128,512]{2,1,0:T(8,128)(2,1)} %copy-done.6, bf16[8,128,512]{2,1,0:T(8,128)(2,1)} %copy-done.21, bf16[8,128,512]{2,1,0:T(8,128)(2,1)} %copy-done.22, ...), custom_call_target="tpu_custom_call" | custom-call | flops 4294967296 | bytes 16777216 | tf_op jit(solution)/shard_map/layer_output/pallas_call | solution.py:607
  308.3 9.0 %collective-permute-done.63 = bf16[8,32,1024]{2,1,0:T(8,128)(2,1)S(1)} collective-permute-done((bf16[8,32,1024]{2,1,0:T(8,128)(2,1)S(1)}, bf16[8,32,1024]{2,1,0:T(8,128)(2,1)S(1)}, u32[]{:S(2)}, u32[]{:S(2)}) %collective-permute-start.63) | collective-permute-done | bytes 524320 | tf_op jit(solution)/shard_map/ppermute | solution.py:57
  321.1 9.5 %collective-permute-done.53 = bf16[8,32,1024]{2,1,0:T(8,128)(2,1)S(1)} collective-permute-done((bf16[8,32,1024]{2,1,0:T(8,128)(2,1)S(1)}, bf16[8,32,1024]{2,1,0:T(8,128)(2,1)S(1)}, u32[]{:S(2)}, u32[]{:S(2)}) %collective-permute-start.53) | collective-permute-done | bytes 524320 | tf_op jit(solution)/shard_map/ppermute | solution.py:57
  346.3 7.2 %collective-permute-done.65 = bf16[2,32,1024]{2,1,0:T(8,128)(2,1)S(1)} collective-permute-done((bf16[2,32,1024]{2,1,0:T(8,128)(2,1)S(1)}, bf16[2,32,1024]{2,1,0:T(8,128)(2,1)S(1)}, u32[]{:S(2)}, u32[]{:S(2)}) %collective-permute-start.65) | collective-permute-done | bytes 131104 | tf_op jit(solution)/shard_map/ppermute | solution.py:57
  363.4 6.7 %collective-permute-done.50 = bf16[2,32,1024]{2,1,0:T(8,128)(2,1)S(1)} collective-permute-done((bf16[2,32,1024]{2,1,0:T(8,128)(2,1)S(1)}, bf16[2,32,1024]{2,1,0:T(8,128)(2,1)S(1)}, u32[]{:S(2)}, u32[]{:S(2)}) %collective-permute-start.50) | collective-permute-done | bytes 131104 | tf_op jit(solution)/shard_map/ppermute | solution.py:57
  375.0 4.8 %collective-permute-done.61 = bf16[1,32,1024]{2,1,0:T(8,128)(2,1)S(1)} collective-permute-done((bf16[1,32,1024]{2,1,0:T(8,128)(2,1)S(1)}, bf16[1,32,1024]{2,1,0:T(8,128)(2,1)S(1)}, u32[]{:S(2)}, u32[]{:S(2)}) %collective-permute-start.61) | collective-permute-done | bytes 65568 | tf_op jit(solution)/shard_map/ppermute | solution.py:57
  399.6 9.1 %collective-permute-done.78 = bf16[8,128,512]{2,1,0:T(8,128)(2,1)S(1)} collective-permute-done((bf16[8,128,512]{2,1,0:T(8,128)(2,1)S(1)}, bf16[8,128,512]{2,1,0:T(8,128)(2,1)S(1)}, u32[]{:S(2)}, u32[]{:S(2)}) %collective-permute-start.78) | collective-permute-done | bytes 1048608 | tf_op jit(solution)/shard_map/ppermute | solution.py:57
  409.7 10.5 %collective-permute-done.83 = bf16[8,128,512]{2,1,0:T(8,128)(2,1)S(1)} collective-permute-done((bf16[8,128,512]{2,1,0:T(8,128)(2,1)S(1)}, bf16[8,128,512]{2,1,0:T(8,128)(2,1)S(1)}, u32[]{:S(2)}, u32[]{:S(2)}) %collective-permute-start.83) | collective-permute-done | bytes 1048608 | tf_op jit(solution)/shard_map/ppermute | solution.py:57
  421.8 15.4 %collective-permute-done.73 = bf16[8,32,2048]{2,1,0:T(8,128)(2,1)S(1)} collective-permute-done((bf16[8,32,2048]{2,1,0:T(8,128)(2,1)S(1)}, bf16[8,32,2048]{2,1,0:T(8,128)(2,1)S(1)}, u32[]{:S(2)}, u32[]{:S(2)}) %collective-permute-start.73) | collective-permute-done | bytes 1048608 | tf_op jit(solution)/shard_map/ppermute | solution.py:57
  438.0 7.7 %collective-permute-done.79 = bf16[4,128,512]{2,1,0:T(8,128)(2,1)S(1)} collective-permute-done((bf16[4,128,512]{2,1,0:T(8,128)(2,1)S(1)}, bf16[4,128,512]{2,1,0:T(8,128)(2,1)S(1)}, u32[]{:S(2)}, u32[]{:S(2)}) %collective-permute-start.79) | collective-permute-done | bytes 524320 | tf_op jit(solution)/shard_map/ppermute | solution.py:57
  453.2 6.5 %collective-permute-done.80 = bf16[2,128,512]{2,1,0:T(8,128)(2,1)S(1)} collective-permute-done((bf16[2,128,512]{2,1,0:T(8,128)(2,1)S(1)}, bf16[2,128,512]{2,1,0:T(8,128)(2,1)S(1)}, u32[]{:S(2)}, u32[]{:S(2)}) %collective-permute-start.80) | collective-permute-done | bytes 262176 | tf_op jit(solution)/shard_map/ppermute | solution.py:57
  466.2 5.5 %collective-permute-done.71 = bf16[1,32,2048]{2,1,0:T(8,128)(2,1)S(1)} collective-permute-done((bf16[1,32,2048]{2,1,0:T(8,128)(2,1)S(1)}, bf16[1,32,2048]{2,1,0:T(8,128)(2,1)S(1)}, u32[]{:S(2)}, u32[]{:S(2)}) %collective-permute-start.71) | collective-permute-done | bytes 131104 | tf_op jit(solution)/shard_map/ppermute | solution.py:57
  (350 shorter events, 182.2 us)
Async XLA Ops:
  29.5 25.0 %collective-permute-start.25 = (bf16[2,32,2048]{2,1,0:T(8,128)(2,1)S(1)}, bf16[2,32,2048]{2,1,0:T(8,128)(2,1)S(1)}, u32[]{:S(2)}, u32[]{:S(2)}) collective-permute-start(bf16[2,32,2048]{2,1,0:T(8,128)(2,1)S(1)} %pad_maximum_fusion.17), channel_id=1, source_target_pairs={{0,2},{1,3},{2,0},{3,1},{4,6},{5,7},{6,4},{7,5},{8,10},{9,11},{10,... | collective-permute-start | bytes 786440 | tf_op jit(solution)/shard_map/ppermute | solution.py:57
  31.4 24.6 %collective-permute-start.31 = (bf16[2,128,512]{2,1,0:T(8,128)(2,1)S(1)}, bf16[2,128,512]{2,1,0:T(8,128)(2,1)S(1)}, u32[]{:S(2)}, u32[]{:S(2)}) collective-permute-start(bf16[2,128,512]{2,1,0:T(8,128)(2,1)S(1)} %pad_maximum_fusion.18), channel_id=1, source_target_pairs={{0,4},{1,5},{2,6},{3,7},{4,0},{5,1},{6,2},{7,3},{8,12},{9,13},{10,... | collective-permute-start | bytes 786440 | tf_op jit(solution)/shard_map/ppermute | solution.py:57
  88.5 33.3 %collective-permute-start.21 = (bf16[8,32,2048]{2,1,0:T(8,128)(2,1)S(1)}, bf16[8,32,2048]{2,1,0:T(8,128)(2,1)}, u32[]{:S(2)}, u32[]{:S(2)}) collective-permute-start(bf16[8,32,2048]{2,1,0:T(8,128)(2,1)S(1)} %pad_maximum_fusion.refs_2_.refs_6_), channel_id=1, source_target_pairs={{0,2},{1,3},{2,0},{3,1},{4,6},{5,7},{6,4},{7,5},{8,10},{9,11},{10,... | collective-permute-start | bytes 3145736 | tf_op jit(solution)/shard_map/ppermute | solution.py:57
  101.1 25.7 %collective-permute-start.27 = (bf16[8,32,2048]{2,1,0:T(8,128)(2,1)S(1)}, bf16[8,32,2048]{2,1,0:T(8,128)(2,1)}, u32[]{:S(2)}, u32[]{:S(2)}) collective-permute-start(bf16[8,32,2048]{2,1,0:T(8,128)(2,1)S(1)} %pad_maximum_fusion.1.refs_6_.refs_10_), channel_id=1, source_target_pairs={{0,4},{1,5},{2,6},{3,7},{4,0},{5,1},{6,2},{7,3},{8,12},{9,13},{10,... | collective-permute-start | bytes 3145736 | tf_op jit(solution)/shard_map/ppermute | solution.py:57
  104.0 26.3 %collective-permute-start.33 = (bf16[8,128,512]{2,1,0:T(8,128)(2,1)S(1)}, bf16[8,128,512]{2,1,0:T(8,128)(2,1)S(1)}, u32[]{:S(2)}, u32[]{:S(2)}) collective-permute-start(bf16[8,128,512]{2,1,0:T(8,128)(2,1)S(1)} %pad_maximum_fusion.2.refs_2_.refs_14_), channel_id=1, source_target_pairs={{0,8},{1,9},{2,10},{3,11},{4,12},{5,13},{6,14},{7,15},{8,0},{9,1},... | collective-permute-start | bytes 3145736 | tf_op jit(solution)/shard_map/ppermute | solution.py:57
  121.7 24.6 %collective-permute-start.39 = (bf16[8,128,512]{2,1,0:T(8,128)(2,1)S(1)}, bf16[8,128,512]{2,1,0:T(8,128)(2,1)}, u32[]{:S(2)}, u32[]{:S(2)}) collective-permute-start(bf16[8,128,512]{2,1,0:T(8,128)(2,1)S(1)} %pad_maximum_fusion.3.refs_6_.refs_18_), channel_id=1, source_target_pairs={{0,2},{1,3},{2,0},{3,1},{4,6},{5,7},{6,4},{7,5},{8,10},{9,11},{10,... | collective-permute-start | bytes 3145736 | tf_op jit(solution)/shard_map/ppermute | solution.py:57
  130.4 44.9 %collective-permute-start.29 = (bf16[8,32,2048]{2,1,0:T(8,128)(2,1)}, bf16[8,32,2048]{2,1,0:T(8,128)(2,1)}, u32[]{:S(2)}, u32[]{:S(2)}) collective-permute-start(bf16[8,32,2048]{2,1,0:T(8,128)(2,1)} %collective-permute-done.27.refs_7_.refs_11_), channel_id=1, source_target_pairs={{0,1},{1,0},{2,3},{3,2},{4,5},{5,4},{6,7},{7,6},{8,9},{9,8},{10,11... | collective-permute-start | bytes 3145736 | tf_op jit(solution)/shard_map/ppermute | solution.py:57
  146.3 50.4 %collective-permute-start.34 = (bf16[8,128,512]{2,1,0:T(8,128)(2,1)S(1)}, bf16[8,128,512]{2,1,0:T(8,128)(2,1)S(1)}, u32[]{:S(2)}, u32[]{:S(2)}) collective-permute-start(bf16[8,128,512]{2,1,0:T(8,128)(2,1)S(1)} %pad_maximum_fusion.2.refs_2_.refs_14_), channel_id=1, source_target_pairs={{0,1},{1,0},{2,3},{3,2},{4,5},{5,4},{6,7},{7,6},{8,9},{9,8},{10,11... | collective-permute-start | bytes 3145736 | tf_op jit(solution)/shard_map/ppermute | solution.py:57
  146.3 50.4 %collective-permute-start.40 = (bf16[8,128,512]{2,1,0:T(8,128)(2,1)S(1)}, bf16[8,128,512]{2,1,0:T(8,128)(2,1)S(1)}, u32[]{:S(2)}, u32[]{:S(2)}) collective-permute-start(bf16[8,128,512]{2,1,0:T(8,128)(2,1)S(1)} %pad_maximum_fusion.3.refs_6_.refs_18_), channel_id=1, source_target_pairs={{0,1},{1,0},{2,3},{3,2},{4,5},{5,4},{6,7},{7,6},{8,9},{9,8},{10,11... | collective-permute-start | bytes 3145736 | tf_op jit(solution)/shard_map/ppermute | solution.py:57
  146.8 49.9 %collective-permute-start.35 = (bf16[8,128,512]{2,1,0:T(8,128)(2,1)S(1)}, bf16[8,128,512]{2,1,0:T(8,128)(2,1)S(1)}, u32[]{:S(2)}, u32[]{:S(2)}) collective-permute-start(bf16[8,128,512]{2,1,0:T(8,128)(2,1)S(1)} %collective-permute-done.33.refs_3_.refs_15_), channel_id=1, source_target_pairs={{0,1},{1,0},{2,3},{3,2},{4,5},{5,4},{6,7},{7,6},{8,9},{9,8},{10,11... | collective-permute-start | bytes 3145736 | tf_op jit(solution)/shard_map/ppermute | solution.py:57
  146.9 49.9 %collective-permute-start.41 = (bf16[8,128,512]{2,1,0:T(8,128)(2,1)}, bf16[8,128,512]{2,1,0:T(8,128)(2,1)S(1)}, u32[]{:S(2)}, u32[]{:S(2)}) collective-permute-start(bf16[8,128,512]{2,1,0:T(8,128)(2,1)} %collective-permute-done.39.refs_7_.refs_19_), channel_id=1, source_target_pairs={{0,1},{1,0},{2,3},{3,2},{4,5},{5,4},{6,7},{7,6},{8,9},{9,8},{10,11... | collective-permute-start | bytes 3145736 | tf_op jit(solution)/shard_map/ppermute | solution.py:57
  230.3 68.4 %collective-permute-start.62 = (bf16[16,32,1024]{2,1,0:T(8,128)(2,1)}, bf16[16,32,1024]{2,1,0:T(8,128)(2,1)}, u32[]{:S(2)}, u32[]{:S(2)}) collective-permute-start(bf16[16,32,1024]{2,1,0:T(8,128)(2,1)} %get-tuple-element.78), channel_id=1, source_target_pairs={{0,1},{1,0},{2,3},{3,2},{4,5},{5,4},{6,7},{7,6},{8,9},{9,8},{10,11... | collective-permute-start | bytes 3145736 | tf_op jit(solution)/shard_map/ppermute | solution.py:57
  269.9 31.1 %collective-permute-start.57 = (bf16[16,32,1024]{2,1,0:T(8,128)(2,1)}, bf16[16,32,1024]{2,1,0:T(8,128)(2,1)}, u32[]{:S(2)}, u32[]{:S(2)}) collective-permute-start(bf16[16,32,1024]{2,1,0:T(8,128)(2,1)} %get-tuple-element.76), channel_id=1, source_target_pairs={{0,1},{1,0},{2,3},{3,2},{4,5},{5,4},{6,7},{7,6},{8,9},{9,8},{10,11... | collective-permute-start | bytes 3145736 | tf_op jit(solution)/shard_map/ppermute | solution.py:57
  278.2 112.6 %collective-permute-start.77 = (bf16[16,128,512]{2,1,0:T(8,128)(2,1)}, bf16[16,128,512]{2,1,0:T(8,128)(2,1)S(1)}, u32[]{:S(2)}, u32[]{:S(2)}) collective-permute-start(bf16[16,128,512]{2,1,0:T(8,128)(2,1)} %get-tuple-element.84), channel_id=1, source_target_pairs={{0,1},{1,0},{2,3},{3,2},{4,5},{5,4},{6,7},{7,6},{8,9},{9,8},{10,11... | collective-permute-start | bytes 6291464 | tf_op jit(solution)/shard_map/ppermute | solution.py:57
  278.2 24.8 %collective-permute-start.52 = (bf16[16,32,1024]{2,1,0:T(8,128)(2,1)}, bf16[16,32,1024]{2,1,0:T(8,128)(2,1)}, u32[]{:S(2)}, u32[]{:S(2)}) collective-permute-start(bf16[16,32,1024]{2,1,0:T(8,128)(2,1)} %get-tuple-element.74), channel_id=1, source_target_pairs={{0,1},{1,0},{2,3},{3,2},{4,5},{5,4},{6,7},{7,6},{8,9},{9,8},{10,11... | collective-permute-start | bytes 3145736 | tf_op jit(solution)/shard_map/ppermute | solution.py:57
  298.7 93.2 %collective-permute-start.82 = (bf16[16,128,512]{2,1,0:T(8,128)(2,1)}, bf16[16,128,512]{2,1,0:T(8,128)(2,1)S(1)}, u32[]{:S(2)}, u32[]{:S(2)}) collective-permute-start(bf16[16,128,512]{2,1,0:T(8,128)(2,1)} %get-tuple-element.86), channel_id=1, source_target_pairs={{0,1},{1,0},{2,3},{3,2},{4,5},{5,4},{6,7},{7,6},{8,9},{9,8},{10,11... | collective-permute-start | bytes 6291464 | tf_op jit(solution)/shard_map/ppermute | solution.py:57
  301.1 93.5 %collective-permute-start.67 = (bf16[16,32,2048]{2,1,0:T(8,128)(2,1)S(1)}, bf16[16,32,2048]{2,1,0:T(8,128)(2,1)S(1)}, u32[]{:S(2)}, u32[]{:S(2)}) collective-permute-start(bf16[16,32,2048]{2,1,0:T(8,128)(2,1)S(1)} %copy-done.20), channel_id=1, source_target_pairs={{0,1},{1,0},{2,3},{3,2},{4,5},{5,4},{6,7},{7,6},{8,9},{9,8},{10,11... | collective-permute-start | bytes 6291464 | tf_op jit(solution)/shard_map/ppermute | solution.py:57
  343.7 52.9 %collective-permute-start.72 = (bf16[16,32,2048]{2,1,0:T(8,128)(2,1)S(1)}, bf16[16,32,2048]{2,1,0:T(8,128)(2,1)S(1)}, u32[]{:S(2)}, u32[]{:S(2)}) collective-permute-start(bf16[16,32,2048]{2,1,0:T(8,128)(2,1)S(1)} %copy-done.19), channel_id=1, source_target_pairs={{0,1},{1,0},{2,3},{3,2},{4,5},{5,4},{6,7},{7,6},{8,9},{9,8},{10,11... | collective-permute-start | bytes 6291464 | tf_op jit(solution)/shard_map/ppermute | solution.py:57
  394.0 26.2 %collective-permute-start.83 = (bf16[8,128,512]{2,1,0:T(8,128)(2,1)S(1)}, bf16[8,128,512]{2,1,0:T(8,128)(2,1)S(1)}, u32[]{:S(2)}, u32[]{:S(2)}) collective-permute-start(bf16[8,128,512]{2,1,0:T(8,128)(2,1)S(1)} %slice.492), channel_id=1, source_target_pairs={{0,4},{1,5},{2,6},{3,7},{4,0},{5,1},{6,2},{7,3},{8,12},{9,13},{10,... | collective-permute-start | bytes 3145736 | tf_op jit(solution)/shard_map/ppermute | solution.py:57
  396.5 24.3 %collective-permute-start.68 = (bf16[8,32,2048]{2,1,0:T(8,128)(2,1)S(1)}, bf16[8,32,2048]{2,1,0:T(8,128)(2,1)S(1)}, u32[]{:S(2)}, u32[]{:S(2)}) collective-permute-start(bf16[8,32,2048]{2,1,0:T(8,128)(2,1)S(1)} %slice.495), channel_id=1, source_target_pairs={{0,8},{1,9},{2,10},{3,11},{4,12},{5,13},{6,14},{7,15},{8,0},{9,1},... | collective-permute-start | bytes 3145736 | tf_op jit(solution)/shard_map/ppermute | solution.py:57
  398.9 38.4 %collective-permute-start.73 = (bf16[8,32,2048]{2,1,0:T(8,128)(2,1)S(1)}, bf16[8,32,2048]{2,1,0:T(8,128)(2,1)S(1)}, u32[]{:S(2)}, u32[]{:S(2)}) collective-permute-start(bf16[8,32,2048]{2,1,0:T(8,128)(2,1)S(1)} %slice.494), channel_id=1, source_target_pairs={{0,4},{1,5},{2,6},{3,7},{4,0},{5,1},{6,2},{7,3},{8,12},{9,13},{10,... | collective-permute-start | bytes 3145736 | tf_op jit(solution)/shard_map/ppermute | solution.py:57
  409.2 36.5 %collective-permute-start.79 = (bf16[4,128,512]{2,1,0:T(8,128)(2,1)S(1)}, bf16[4,128,512]{2,1,0:T(8,128)(2,1)S(1)}, u32[]{:S(2)}, u32[]{:S(2)}) collective-permute-start(bf16[4,128,512]{2,1,0:T(8,128)(2,1)S(1)} %slice.497), channel_id=1, source_target_pairs={{0,4},{1,5},{2,6},{3,7},{4,0},{5,1},{6,2},{7,3},{8,12},{9,13},{10,... | collective-permute-start | bytes 1572872 | tf_op jit(solution)/shard_map/ppermute | solution.py:57
  420.7 25.6 %collective-permute-start.84 = (bf16[4,128,512]{2,1,0:T(8,128)(2,1)S(1)}, bf16[4,128,512]{2,1,0:T(8,128)(2,1)S(1)}, u32[]{:S(2)}, u32[]{:S(2)}) collective-permute-start(bf16[4,128,512]{2,1,0:T(8,128)(2,1)S(1)} %slice.496), channel_id=1, source_target_pairs={{0,8},{1,9},{2,10},{3,11},{4,12},{5,13},{6,14},{7,15},{8,0},{9,1},... | collective-permute-start | bytes 1572872 | tf_op jit(solution)/shard_map/ppermute | solution.py:57
  421.1 27.1 %collective-permute-start.69 = (bf16[4,32,2048]{2,1,0:T(8,128)(2,1)S(1)}, bf16[4,32,2048]{2,1,0:T(8,128)(2,1)S(1)}, u32[]{:S(2)}, u32[]{:S(2)}) collective-permute-start(bf16[4,32,2048]{2,1,0:T(8,128)(2,1)S(1)} %slice.499), channel_id=1, source_target_pairs={{0,2},{1,3},{2,0},{3,1},{4,6},{5,7},{6,4},{7,5},{8,10},{9,11},{10,... | collective-permute-start | bytes 1572872 | tf_op jit(solution)/shard_map/ppermute | solution.py:57
  (97 other events, 1336.0 us)
